TPU v7x, 32 devices: a whole 2x2x4 slice. The times are simulated.
32 devices in a mesh: dom: 8 (over y, x, core), col: 4 (over z).
Axes of the slice: x: 2, y: 2, z: 4, core: 2. Of those that a mesh axis runs over, the one named last changes fastest.
Arguments:
- basis_panel: bfloat16 [256, 163840], P('col', 'dom'), may hold values from -12 to 12
- jacobian: bfloat16 [2, 320, 16384], P(None, None, 'dom'), may hold values from -0.25 to 0.25
- neighbors: int32 [512, 2], P('dom'), may hold values from 0 to 63
- sample_rows: int32 [16384], P('dom'), may hold values from 0 to 8191, as said below
- residual_parts: float32 [16384], P('dom'), may hold values from -48 to 48
Outputs:
- jacobian_basis: float32 [256, 8192], P('col', 'dom')
- sampled_residual: float32 [8192], P('dom')
- reduced_step: float32 [256], P('col')
Inputs may be any that keep to these rules, and one draw needn't show every extreme that they name: `sample_rows`: for each index d of dom, its 2048 entries name each of its own rows d * 1024 to d * 1024 + 1023 exactly once; the other 1024 entries name rows owned by the 7 indices d + 1 to d + 7 of dom, cyclically, at most 256 to any one of them and exactly 256 to one of them. `neighbors`: each entry is an element of the same index of dom, counted from that index's first element.
All inputs are finite; a program needn't handle non-finite values.
Results may differ from a plain program's by a relative error of at most 0.0003.
Values sent between devices are 32-bit elements; how exact they have to be, the bound alone decides.
A program may use at most 64 MiB of HBM per device.

v0:
```python
import jax
import jax.numpy as jnp
from jax import lax
from jax.sharding import PartitionSpec as P

NODE = 320
NB = 2
RS = 32
ROWS_DEV = 1024
CAP = 256


def element_products(basis_panel, jacobian, neighbors):
    panel_width = basis_panel.shape[0]
    element_count = neighbors.shape[0]
    panels = basis_panel.reshape(panel_width, element_count, NODE)
    blocks = jacobian.reshape(NB, NODE, element_count, RS)
    summed = jnp.zeros((panel_width, element_count, RS), jnp.float32)
    for coupled in range(NB):
        picked = jnp.take(panels, neighbors[:, coupled], axis=1)
        summed = summed + jnp.einsum(
            "cep,per->cer", picked, blocks[coupled], preferred_element_type=jnp.float32
        )
    return summed.reshape(panel_width, element_count * RS)


def body(basis_panel, jacobian, neighbors, sample_rows, residual_parts):
    dom_count = lax.axis_size("dom")
    self_index = lax.axis_index("dom")
    partial_value = element_products(basis_panel, jacobian, neighbors)
    panel_width = partial_value.shape[0]
    owners = sample_rows // ROWS_DEV
    local_rows = sample_rows % ROWS_DEV
    is_local = owners == self_index
    own_rows = jnp.where(is_local, local_rows, ROWS_DEV)
    jacobian_basis = (
        jnp.zeros((panel_width, ROWS_DEV), jnp.float32)
        .at[:, own_rows]
        .add(partial_value, mode="drop")
    )
    sampled_residual = (
        jnp.zeros((ROWS_DEV,), jnp.float32).at[own_rows].add(residual_parts, mode="drop")
    )
    matches = (owners[None, :] == jnp.arange(dom_count, dtype=jnp.int32)[:, None]).astype(jnp.int32)
    ranking = jnp.sum(matches * (jnp.cumsum(matches, axis=1) - 1), axis=0)
    row_values = local_rows.astype(jnp.float32)
    target_slot = jnp.where(is_local, dom_count * CAP, owners * CAP + ranking)
    send_values = (
        jnp.zeros((panel_width, dom_count * CAP), jnp.float32)
        .at[:, target_slot]
        .set(partial_value, mode="drop")
        .reshape(panel_width, dom_count, CAP)
    )
    send_residual = (
        jnp.zeros((dom_count * CAP,), jnp.float32)
        .at[target_slot]
        .set(residual_parts, mode="drop")
        .reshape(1, dom_count, CAP)
    )
    send_rows = (
        jnp.full((dom_count * CAP,), float(ROWS_DEV), jnp.float32)
        .at[target_slot]
        .set(row_values, mode="drop")
        .reshape(1, dom_count, CAP)
    )
    arrived_values, arrived_residual, arrived_rows = (
        lax.all_to_all(send_values, "dom", split_axis=1, concat_axis=1, tiled=True),
        lax.all_to_all(send_residual, "dom", split_axis=1, concat_axis=1, tiled=True),
        lax.all_to_all(send_rows, "dom", split_axis=1, concat_axis=1, tiled=True),
    )
    landing = arrived_rows.reshape(-1).astype(jnp.int32)
    jacobian_basis = jacobian_basis.at[:, landing].add(
        arrived_values.reshape(panel_width, -1), mode="drop"
    )
    sampled_residual = sampled_residual.at[landing].add(arrived_residual.reshape(-1), mode="drop")
    gram_panel = jnp.einsum(
        "cr,kr->ck",
        jacobian_basis,
        lax.all_gather(jacobian_basis, "col", axis=0, tiled=True),
        precision=lax.Precision.HIGHEST,
        preferred_element_type=jnp.float32,
    )
    gradient_panel = jnp.einsum(
        "cr,r->c", jacobian_basis, sampled_residual, precision=lax.Precision.HIGHEST
    )
    gram_panel, gradient_panel = lax.psum((gram_panel, gradient_panel), "dom")
    gram_matrix, gradient = (
        lax.all_gather(gram_panel, "col", axis=0, tiled=True),
        lax.all_gather(gradient_panel, "col", axis=0, tiled=True),
    )
    factor = jnp.linalg.cholesky(gram_matrix)
    forward = lax.linalg.triangular_solve(factor, gradient[:, None], left_side=True, lower=True)
    backward = lax.linalg.triangular_solve(
        factor, forward, left_side=True, lower=True, transpose_a=True
    )
    full_step = -backward[:, 0]
    reduced_step = lax.dynamic_slice_in_dim(
        full_step, lax.axis_index("col") * panel_width, panel_width
    )
    return (jacobian_basis, sampled_residual, reduced_step)


def solution(mesh):
    placed = (P("col", "dom"), P(None, None, "dom"), P("dom", None), P("dom"), P("dom"))
    return jax.shard_map(
        body,
        mesh=mesh,
        in_specs=placed,
        out_specs=(P("col", "dom"), P("dom"), P("col")),
        check_vma=False,
    )
```

profile of v0, /device:TPU:0, one launch (start us, length us, event | category | flops | bytes accessed | tf_op | source)
XLA Modules:
  0.0 269.6 jit_solution(11350941554137800670)
XLA Ops:
  11.5 8.6 %scatter_custom_fusion.1 = f32[2048]{0:T(1024)} fusion(s32[2048]{0:T(1024)S(1)} %compare_select_fusion.1, f32[2048]{0:T(1024)S(1)} %get-tuple-element.47, f32[]{:T(128)} %constant.144.clone.1), kind=kCustom, calls=%fused_computation.75 | custom fusion | bytes 8196 | tf_op jit(solution)/shard_map/scatter | solution.py:63
  20.1 5.2 %all-to-all-start = ((f32[1,8,256]{2,0,1:T(1,128)}), f32[1,8,256]{2,0,1:T(1,128)S(1)}, u32[]{:S(2)}, u32[]{:S(2)}) async-start(f32[1,8,256]{2,0,1:T(1,128)} %bitcast.11), calls=%async_computation | async-start | bytes 16384 | tf_op jit(solution)/shard_map/all_to_all | solution.py:69
  25.3 3.0 %fusion.47 = (bf16[1,320,2048]{2,1,0:T(8,128)(2,1)}, bf16[1,320,2048]{2,1,0:T(8,128)(2,1)S(1)}) fusion(bf16[2,320,2048]{2,1,0:T(8,128)(2,1)} %param.8), kind=kLoop, calls=%fused_computation.101 | loop fusion | bytes 5242880 | tf_op jit(solution)/shard_map/slice | solution.py:22
  29.9 6.2 %reshape.129 = bf16[64,64,320]{2,1,0:T(8,128)(2,1)} reshape(bf16[64,20480]{1,0:T(8,128)(2,1)} %param.7) | data formatting | bytes 5242880 | tf_op jit(solution)/shard_map/reshape | solution.py:16
  36.1 3.8 %copy.33 = bf16[64,64,320]{2,0,1:T(8,128)(2,1)S(1)} copy(bf16[64,64,320]{2,1,0:T(8,128)(2,1)} %reshape.129) | data formatting | bytes 5242880 | tf_op jit(solution)/shard_map/reshape | solution.py:16
  47.8 3.8 %fusion = f32[64,64,32]{1,2,0:T(8,128)S(1)} fusion(bf16[320,64,32]{0,2,1:T(8,128)(2,1)} %bitcast.125, bf16[64,64,320]{2,1,0:T(8,128)(2,1)} %gather_fusion.1, pred[64]{0:T(512)(128)(4,1)S(1)} %get-tuple-element.50), kind=kOutput, calls=%fused_computation.11 | convolution fusion | flops 85196800 | bytes 4456512 | tf_op jit(solution)/shard_map/cep,per->cer/dot_general | solution.py:21
  52.9 5.8 %scatter_custom_fusion.2 = f32[64,2048]{0,1:T(8,128)S(1)} fusion(s32[2048]{0:T(1024)S(1)} %compare_select_fusion.1, f32[2048,64]{1,0:T(8,128)S(1)} %bitcast.132, f32[]{:T(128)} %constant.135.clone.1), kind=kCustom, calls=%fused_computation.33 | custom fusion | bytes 524292 | tf_op jit(solution)/shard_map/scatter | solution.py:51
  59.9 4.2 %all-to-all-start.1 = ((f32[64,8,256]{2,0,1:T(8,128)}), f32[64,8,256]{2,0,1:T(8,128)S(1)}, u32[]{:S(2)}, u32[]{:S(2)}) async-start(f32[64,8,256]{2,0,1:T(8,128)} %copy.37), calls=%async_computation.1 | async-start | bytes 1048576 | tf_op jit(solution)/shard_map/all_to_all | solution.py:67
  64.3 11.6 %scatter_custom_fusion = f32[64,1024]{0,1:T(8,128)S(1)} fusion(s32[2048]{0:T(1024)S(1)} %get-tuple-element.49, f32[2048,64]{1,0:T(8,128)S(1)} %bitcast.133, f32[]{:T(128)} %constant.135.clone.1), kind=kCustom, calls=%fused_computation.39 | custom fusion | flops 131072 | bytes 262148 | tf_op jit(solution)/shard_map/scatter-add | solution.py:39
  76.4 11.7 %scatter_fusion = f32[64,1024]{0,1:T(8,128)S(1)} fusion(f32[64,1024]{0,1:T(8,128)S(1)} %scatter_custom_fusion, s32[2048]{0:T(1024)S(1)} %bitcast.127, f32[2048,64]{1,0:T(8,128)S(1)} %copy.39), kind=kCustom, calls=%fused_computation.5 | custom fusion | flops 131072 | bytes 1581056 | tf_op jit(solution)/shard_map/scatter-add | solution.py:72
  89.0 8.8 %scatter_custom_fusion.5 = f32[2048]{0:T(1024)} fusion(s32[2048]{0:T(1024)S(1)} %compare_select_fusion.1, f32[2048]{0:T(1024)} %param.11, f32[]{:T(128)} %constant.135.clone.1), kind=kCustom, calls=%fused_computation.73 | custom fusion | bytes 8704 | tf_op jit(solution)/shard_map/scatter | solution.py:57
  97.7 4.0 %all-to-all-start.2 = ((f32[1,8,256]{2,0,1:T(1,128)}), f32[1,8,256]{2,0,1:T(1,128)S(1)}, u32[]{:S(2)}, u32[]{:S(2)}) async-start(f32[1,8,256]{2,0,1:T(1,128)} %bitcast.18), calls=%async_computation.2 | async-start | bytes 16384 | tf_op jit(solution)/shard_map/all_to_all | solution.py:68
  101.8 11.7 %scatter_custom_fusion.4 = f32[1024]{0:T(1024)S(1)} fusion(s32[2048]{0:T(1024)S(1)} %get-tuple-element.49, f32[2048]{0:T(1024)} %param.11, f32[]{:T(128)} %constant.135.clone.1), kind=kCustom, calls=%fused_computation.80 | custom fusion | flops 2048 | bytes 4608 | tf_op jit(solution)/shard_map/scatter-add | solution.py:42
  114.7 13.2 %scatter_fusion.1 = f32[1024]{0:T(1024)S(1)} fusion(f32[1024]{0:T(1024)S(1)} %scatter_custom_fusion.4, s32[2048]{0:T(1024)S(1)} %bitcast.128, f32[2048]{0:T(1024)S(1)} %bitcast.129), kind=kCustom, calls=%fused_computation.8 | custom fusion | flops 2048 | bytes 32768 | tf_op jit(solution)/shard_map/scatter-add | solution.py:75
  128.0 2.9 %fusion.48 = f32[64,256]{1,0:T(8,128)} fusion(f32[64,1024]{0,1:T(8,128)S(1)} %scatter_fusion, f32[256,1024]{1,0:T(8,128)} %all-gather.2.cloned.1.call-done), kind=kOutput, calls=%fused_computation.102 | convolution fusion | flops 201326592 | bytes 1376256 | tf_op jit(solution)/shard_map/cr,kr->ck/dot_general | solution.py:76
  131.3 14.0 %psum.15 = f32[64]{0:T(128)S(1)} all-reduce(f32[64]{0:T(128)S(1)} %convolution_bitcast_fusion.5), channel_id=1, replica_groups=mesh['dom'=8,'col'=4] {'dom'}, use_global_device_ids=true, to_apply=%region_15.17 | all-reduce | flops 64 | bytes 512 | tf_op jit(solution)/shard_map/psum | solution.py:86
  145.5 11.9 %all-reduce.1 = f32[256]{0:T(256)S(1)} all-reduce(f32[256]{0:T(256)S(1)} %dynamic-update-slice.11), channel_id=1, replica_groups=mesh['dom'=8,'col'=4] {'col'}, use_global_device_ids=true, to_apply=%add.1 | all-reduce | flops 256 | bytes 2048
  157.4 28.5 %all-reduce.4.cloned.1.call-done = f32[64,256]{1,0:T(8,128)} async-done(((f32[64,256]{1,0:T(8,128)}), f32[64,256]{1,0:T(8,128)}) %all-reduce.4.cloned.1.call-update) | async-done | bytes 65552 | tf_op jit(solution)/shard_map/psum | solution.py:86
  185.9 14.3 %all_gather.10 = f32[256,256]{1,0:T(8,128)S(1)} all-gather(f32[64,256]{1,0:T(8,128)} %all-reduce.4.cloned.1.call-done), channel_id=1, replica_groups=mesh['dom'=8,'col'=4] {'col'}, dimensions={0}, use_global_device_ids=true | all-gather | bytes 327680 | tf_op jit(solution)/shard_map/all_gather | solution.py:88
  200.4 11.7 %cholesky.50 = f32[128,128]{1,0:T(8,128)S(1)} custom-call(f32[128,128]{1,0:T(8,128)S(1)} %cholesky.118), custom_call_target="Cholesky" | custom-call | tf_op jit(solution)/shard_map/jit(cholesky)/cholesky | solution.py:91
  212.2 9.8 %custom-call.16 = f32[1,128,128]{1,2,0:T(8,128)S(1)} custom-call(f32[1,128,128]{2,1,0:T(8,128)S(1)} %get-tuple-element.46), custom_call_target="InvertDiagBlocksLowerTriangular" | custom-call | tf_op jit(solution)/shard_map/jit(cholesky)/cholesky | solution.py:91
  222.5 11.7 %cholesky.105 = f32[128,128]{1,0:T(8,128)S(1)} custom-call(f32[128,128]{1,0:T(8,128)S(1)} %convolution_subtract_fusion), custom_call_target="Cholesky" | custom-call | tf_op jit(solution)/shard_map/jit(cholesky)/cholesky | solution.py:91
  237.0 4.3 %while.1 = (s32[]{:T(128)}, f32[256,256]{1,0:T(8,128)S(1)}, s32[2,2]{1,0:T(2,128)S(1)}, f32[2,128,128]{2,1,0:T(8,128)S(1)}, s32[]{:T(128)}) while((s32[]{:T(128)}, f32[256,256]{1,0:T(8,128)S(1)}, s32[2,2]{1,0:T(2,128)S(1)}, f32[2,128,128]{2,1,0:T(8,128)S(1)}, s32[]{:T(128)}) %tuple.40), condition=%wide.while_cond, body=%wide.while_body.sunk | while | flops 2 | bytes 131189 | solution.py:93
  241.3 19.7 %custom-call.17 = f32[2,128,128]{1,2,0:T(8,128)S(1)} custom-call(f32[2,128,128]{2,1,0:T(8,128)S(1)} %get-tuple-element.11), custom_call_target="InvertDiagBlocksLowerTriangular" | custom-call | tf_op jit(solution)/shard_map/triangular_solve | solution.py:93
  (69 shorter events, 26.9 us)
Async XLA Ops:
  20.1 39.8 %all-to-all-start = ((f32[1,8,256]{2,0,1:T(1,128)}), f32[1,8,256]{2,0,1:T(1,128)S(1)}, u32[]{:S(2)}, u32[]{:S(2)}) async-start(f32[1,8,256]{2,0,1:T(1,128)} %bitcast.11), calls=%async_computation | async-start | bytes 16384 | tf_op jit(solution)/shard_map/all_to_all | solution.py:69
  36.1 3.8 %copy-start.3 = (s32[64,2]{0,1:T(2,128)S(1)}, s32[64,2]{0,1:T(2,128)}, u32[]{:S(2)}) copy-start(s32[64,2]{0,1:T(2,128)} %param.9) | copy-start | bytes 1540
  47.8 3.8 %copy-start.1 = (bf16[64,64,320]{2,1,0:T(8,128)(2,1)S(1)}, bf16[64,64,320]{2,1,0:T(8,128)(2,1)}, u32[]{:S(2)}) copy-start(bf16[64,64,320]{2,1,0:T(8,128)(2,1)} %gather_fusion) | copy-start | bytes 7864324
  47.8 3.8 %copy-start.2 = (bf16[1,320,2048]{1,2,0:T(8,128)(2,1)S(1)}, bf16[1,320,2048]{1,2,0:T(8,128)(2,1)}, u32[]{:S(2)}) copy-start(bf16[1,320,2048]{1,2,0:T(8,128)(2,1)} %copy.34) | copy-start | bytes 3932164
  59.9 16.1 %all-to-all-start.1 = ((f32[64,8,256]{2,0,1:T(8,128)}), f32[64,8,256]{2,0,1:T(8,128)S(1)}, u32[]{:S(2)}, u32[]{:S(2)}) async-start(f32[64,8,256]{2,0,1:T(8,128)} %copy.37), calls=%async_computation.1 | async-start | bytes 1048576 | tf_op jit(solution)/shard_map/all_to_all | solution.py:67
  64.1 63.9 %all-gather.2.cloned.1.call-start = ((), (), s32[]{:S(2)}) async-start(), calls=%async_computation.3 | async-start | bytes 1310720 | tf_op jit(solution)/shard_map/all_gather | solution.py:79
  76.4 37.1 %copy-start.4 = (u32[32]{0:T(128)S(1)}, u32[32]{0:T(128)}, u32[]{:S(2)}) copy-start(u32[32]{0:T(128)} %constant.171) | copy-start | bytes 388
  97.7 17.0 %all-to-all-start.2 = ((f32[1,8,256]{2,0,1:T(1,128)}), f32[1,8,256]{2,0,1:T(1,128)S(1)}, u32[]{:S(2)}, u32[]{:S(2)}) async-start(f32[1,8,256]{2,0,1:T(1,128)} %bitcast.18), calls=%async_computation.2 | async-start | bytes 16384 | tf_op jit(solution)/shard_map/all_to_all | solution.py:68
  101.7 84.2 %all-reduce.4.cloned.1.call-start = ((), (), s32[]{:S(2)}) async-start(), calls=%async_computation.4 | async-start | bytes 131072 | tf_op jit(solution)/shard_map/psum | solution.py:86
  127.9 109.0 %copy-start = (f32[1024]{0:T(1024)}, f32[1024]{0:T(1024)S(1)}, u32[]{:S(2)}) copy-start(f32[1024]{0:T(1024)S(1)} %scatter_fusion.1) | copy-start | bytes 12292
Sparse Core Ops, SparseCore 0:
  89.1 29.4 all-gather.1
  131.0 54.8 all-reduce.3
where the time goes:
time: 270 us
  other arithmetic  107 us (40%)
  local copies, waits for them, and re-layouts  53.5 us (20%)
  blocking collectives  40.2 us (15%)
  waiting for transfers between devices  28.6 us (11%)
  between operations  16.2 us (6%)
  starting transfers between devices  13.6 us (5%)
  matrix products  9.92 us (4%)
    another operation x7, other arithmetic, body(): factor = jnp.linalg.cholesky(gram_matrix)  34.7 us
    psum x1, waiting for transfers between devices, body(): gram_panel, gradient_panel = lax.psum((gram_panel, gradient_panel), 'dom')  28.5 us
    another operation x3, other arithmetic, body(): lax.linalg.triangular_solve(factor, forward, left_side=True, lower=True,...  19.7 us
    all_gather x1, blocking collectives, body(): lax.all_gather(gram_panel, 'col', axis=0, tiled=True)  14.3 us
    psum x1, blocking collectives, body(): gram_panel, gradient_panel = lax.psum((gram_panel, gradient_panel), 'dom')  14 us
    scatter-add x1, other arithmetic, body(): sampled_residual.at[landing].add(arrived_residual.reshape(-1), mode='drop')  13.2 us
    unnamed x1, blocking collectives  11.9 us
    scatter-add x1, other arithmetic, body(): jacobian_basis.at[:, landing]  11.7 us
  transfers between devices with their start and end apart: 5, of which 1 were waited for; matrix products, arithmetic and copies ran while one was open for 30% of the time, Pallas kernels for 0%

commit v1 on v0

--- a/solution.py
+++ b/solution.py
@@ -8,6 +8,28 @@
 RS = 32
 ROWS_DEV = 1024
 CAP = 256
+
+
+def laid_out(blocks, dim):
+    blocks = jnp.moveaxis(blocks, 0, dim)
+    shape = blocks.shape
+    return blocks.reshape(*shape[:dim], shape[dim] * shape[dim + 1], *shape[dim + 2 :])
+
+
+def ring_gather(x, axis, dim):
+    peers = lax.axis_size(axis)
+    pairs = [(i, (i + 1) % peers) for i in range(peers)]
+    back = [(b, a) for a, b in pairs]
+    lower, upper = ([], [])
+    for step in range(peers - 1):
+        if step % 2 == 0:
+            lower.append(lax.ppermute(lower[-1] if lower else x, axis, pairs))
+        else:
+            upper.append(lax.ppermute(upper[-1] if upper else x, axis, back))
+    blocks = jnp.stack([*lower[::-1], x, *upper])
+    shift = lax.axis_index(axis) - len(lower)
+    blocks = blocks[(jnp.arange(peers) - shift) % peers]
+    return laid_out(blocks, dim)
 
 
 def element_products(basis_panel, jacobian, neighbors):
@@ -85,7 +107,7 @@
     )
     gram_panel, gradient_panel = lax.psum((gram_panel, gradient_panel), "dom")
     gram_matrix, gradient = (
-        lax.all_gather(gram_panel, "col", axis=0, tiled=True),
+        ring_gather(gram_panel, "col", 0),
         lax.all_gather(gradient_panel, "col", axis=0, tiled=True),
     )
     factor = jnp.linalg.cholesky(gram_matrix)

time: 270 us -> 300 us (1.11)
  waiting for transfers between devices: 28.6 us -> 69.6 us
  blocking collectives: 40.2 us -> 24.2 us
  starting transfers between devices: 13.6 us -> 17.5 us
    psum x1, waiting for transfers between devices: 28.5 us -> 52.7 us  [body(): gram_panel, gradient_panel = lax.psum((gram_panel, gradient_panel), 'dom')]
    all_gather x1, waiting for transfers between devices: 0.02 us -> 16.8 us  [body(): lax.all_gather(jacobian_basis, 'col', axis=0, tiled=True)]
    all_gather x1 -> x0, blocking collectives: 14.3 us -> none  [body(): lax.all_gather(gram_panel, 'col', axis=0, tiled=True)]
    ppermute x0 -> x3, starting transfers between devices: none -> 3.88 us  [the longest x1 2.39 us: ring_gather(): upper.append(lax.ppermute(upper[-1] if upper else x, axis, back))]
  transfers between devices with their start and end apart: 5 -> 8, of which waited for: 1 -> 2; matrix products, arithmetic and copies ran while one was open for 30% -> 28% of each run, Pallas kernels for 0% -> 0%
where the time goes in v1:
time: 300 us; the launch traced here: 299 us
  other arithmetic  107 us (36%)
  waiting for transfers between devices  69.6 us (23%)
  local copies, waits for them, and re-layouts  54.1 us (18%)
  blocking collectives  24.2 us (8%)
  starting transfers between devices  17.5 us (6%)
  between operations  16.3 us (5%)
  matrix products  9.91 us (3%)
    psum x1, waiting for transfers between devices, body(): gram_panel, gradient_panel = lax.psum((gram_panel, gradient_panel), 'dom')  52.7 us
    another operation x7, other arithmetic, body(): factor = jnp.linalg.cholesky(gram_matrix)  34.7 us
    another operation x3, other arithmetic, body(): lax.linalg.triangular_solve(factor, forward, left_side=True, lower=True,...  20 us
    all_gather x1, waiting for transfers between devices, body(): lax.all_gather(jacobian_basis, 'col', axis=0, tiled=True)  16.8 us
    scatter-add x1, other arithmetic, body(): sampled_residual.at[landing].add(arrived_residual.reshape(-1), mode='drop')  13.2 us
    unnamed x1, blocking collectives  12.4 us
    psum x1, blocking collectives, body(): gram_panel, gradient_panel = lax.psum((gram_panel, gradient_panel), 'dom')  11.8 us
    scatter-add x1, other arithmetic, body(): jacobian_basis.at[:, landing]  11.7 us
  transfers between devices with their start and end apart: 8, of which 2 were waited for; matrix products, arithmetic and copies ran while one was open for 28% of the time, Pallas kernels for 0%

profile of v1, /device:TPU:0, one launch (start us, length us, event | category | flops | bytes accessed | tf_op | source)
XLA Modules:
  0.0 299.1 jit_solution(14008856613799684210)
XLA Ops:
  11.5 8.6 %scatter_custom_fusion.1 = f32[2048]{0:T(1024)} fusion(s32[2048]{0:T(1024)S(1)} %compare_select_fusion.1, f32[2048]{0:T(1024)S(1)} %get-tuple-element.47, f32[]{:T(128)} %constant.160.clone.1), kind=kCustom, calls=%fused_computation.78 | custom fusion | bytes 8196 | tf_op jit(solution)/shard_map/scatter | solution.py:85
  20.1 5.2 %all-to-all-start = ((f32[1,8,256]{2,0,1:T(1,128)}), f32[1,8,256]{2,0,1:T(1,128)S(1)}, u32[]{:S(2)}, u32[]{:S(2)}) async-start(f32[1,8,256]{2,0,1:T(1,128)} %bitcast.11), calls=%async_computation | async-start | bytes 16384 | tf_op jit(solution)/shard_map/all_to_all | solution.py:91
  25.3 3.0 %fusion.49 = (bf16[1,320,2048]{2,1,0:T(8,128)(2,1)}, bf16[1,320,2048]{2,1,0:T(8,128)(2,1)S(1)}) fusion(bf16[2,320,2048]{2,1,0:T(8,128)(2,1)} %param.8), kind=kLoop, calls=%fused_computation.110 | loop fusion | bytes 5242880 | tf_op jit(solution)/shard_map/slice | solution.py:44
  29.9 6.2 %reshape.181 = bf16[64,64,320]{2,1,0:T(8,128)(2,1)} reshape(bf16[64,20480]{1,0:T(8,128)(2,1)} %param.7) | data formatting | bytes 5242880 | tf_op jit(solution)/shard_map/reshape | solution.py:38
  36.1 3.8 %copy.31 = bf16[64,64,320]{2,0,1:T(8,128)(2,1)S(1)} copy(bf16[64,64,320]{2,1,0:T(8,128)(2,1)} %reshape.181) | data formatting | bytes 5242880 | tf_op jit(solution)/shard_map/reshape | solution.py:38
  47.8 3.8 %fusion = f32[64,64,32]{1,2,0:T(8,128)S(1)} fusion(bf16[320,64,32]{0,2,1:T(8,128)(2,1)} %bitcast.134, bf16[64,64,320]{2,1,0:T(8,128)(2,1)} %gather_fusion.2, pred[64]{0:T(512)(128)(4,1)S(1)} %get-tuple-element.50), kind=kOutput, calls=%fused_computation.12 | convolution fusion | flops 85196800 | bytes 4456512 | tf_op jit(solution)/shard_map/cep,per->cer/dot_general | solution.py:43
  52.9 5.8 %scatter_custom_fusion.2 = f32[64,2048]{0,1:T(8,128)S(1)} fusion(s32[2048]{0:T(1024)S(1)} %compare_select_fusion.1, f32[2048,64]{1,0:T(8,128)S(1)} %bitcast.145, f32[]{:T(128)} %constant.151.clone.1), kind=kCustom, calls=%fused_computation.34 | custom fusion | bytes 524292 | tf_op jit(solution)/shard_map/scatter | solution.py:73
  59.9 4.2 %all-to-all-start.1 = ((f32[64,8,256]{2,0,1:T(8,128)}), f32[64,8,256]{2,0,1:T(8,128)S(1)}, u32[]{:S(2)}, u32[]{:S(2)}) async-start(f32[64,8,256]{2,0,1:T(8,128)} %copy.35), calls=%async_computation.1 | async-start | bytes 1048576 | tf_op jit(solution)/shard_map/all_to_all | solution.py:89
  64.3 11.6 %scatter_custom_fusion = f32[64,1024]{0,1:T(8,128)S(1)} fusion(s32[2048]{0:T(1024)S(1)} %get-tuple-element.49, f32[2048,64]{1,0:T(8,128)S(1)} %bitcast.146, f32[]{:T(128)} %constant.151.clone.1), kind=kCustom, calls=%fused_computation.41 | custom fusion | flops 131072 | bytes 262148 | tf_op jit(solution)/shard_map/scatter-add | solution.py:61
  76.4 11.7 %scatter_fusion = f32[64,1024]{0,1:T(8,128)S(1)} fusion(f32[64,1024]{0,1:T(8,128)S(1)} %scatter_custom_fusion, s32[2048]{0:T(1024)S(1)} %bitcast.136, f32[2048,64]{1,0:T(8,128)S(1)} %copy.37), kind=kCustom, calls=%fused_computation.6 | custom fusion | flops 131072 | bytes 1581056 | tf_op jit(solution)/shard_map/scatter-add | solution.py:94
  89.0 8.8 %scatter_custom_fusion.5 = f32[2048]{0:T(1024)} fusion(s32[2048]{0:T(1024)S(1)} %compare_select_fusion.1, f32[2048]{0:T(1024)} %param.11, f32[]{:T(128)} %constant.151.clone.1), kind=kCustom, calls=%fused_computation.76 | custom fusion | bytes 8704 | tf_op jit(solution)/shard_map/scatter | solution.py:79
  97.8 4.0 %all-to-all-start.2 = ((f32[1,8,256]{2,0,1:T(1,128)}), f32[1,8,256]{2,0,1:T(1,128)S(1)}, u32[]{:S(2)}, u32[]{:S(2)}) async-start(f32[1,8,256]{2,0,1:T(1,128)} %bitcast.18), calls=%async_computation.2 | async-start | bytes 16384 | tf_op jit(solution)/shard_map/all_to_all | solution.py:90
  101.8 16.8 %all-gather.2.cloned.1.call-done = f32[256,1024]{1,0:T(8,128)} async-done(((f32[64,1024]{1,0:T(8,128)}), f32[256,1024]{1,0:T(8,128)}) %all-gather.2.cloned.1.call-update) | async-done | bytes 1048592 | tf_op jit(solution)/shard_map/all_gather | solution.py:101
  118.6 2.9 fusion.50
  121.5 52.7 %all-reduce.4.cloned.1.call-done = f32[64,256]{1,0:T(8,128)} async-done(((f32[64,256]{1,0:T(8,128)}), f32[64,256]{1,0:T(8,128)}) %all-reduce.4.cloned.1.call-update) | async-done | bytes 65552 | tf_op jit(solution)/shard_map/psum | solution.py:108
  175.8 11.7 %scatter_custom_fusion.4 = f32[1024]{0:T(1024)S(1)} fusion(s32[2048]{0:T(1024)S(1)} %get-tuple-element.49, f32[2048]{0:T(1024)} %param.11, f32[]{:T(128)} %constant.151.clone.1), kind=kCustom, calls=%fused_computation.86 | custom fusion | flops 2048 | bytes 4608 | tf_op jit(solution)/shard_map/scatter-add | solution.py:64
  188.7 13.2 %scatter_fusion.1 = f32[1024]{0:T(1024)S(1)} fusion(f32[1024]{0:T(1024)S(1)} %scatter_custom_fusion.4, s32[2048]{0:T(1024)S(1)} %bitcast.137, f32[2048]{0:T(1024)S(1)} %bitcast.142), kind=kCustom, calls=%fused_computation.9 | custom fusion | flops 2048 | bytes 32768 | tf_op jit(solution)/shard_map/scatter-add | solution.py:97
  204.7 11.8 %psum.15 = f32[64]{0:T(128)S(1)} all-reduce(f32[64]{0:T(128)S(1)} %convolution_bitcast_fusion.5), channel_id=1, replica_groups=mesh['dom'=8,'col'=4] {'dom'}, use_global_device_ids=true, to_apply=%region_15.17 | all-reduce | flops 64 | bytes 512 | tf_op jit(solution)/shard_map/psum | solution.py:108
  216.8 12.4 %all-reduce.1 = f32[256]{0:T(256)S(1)} all-reduce(f32[256]{0:T(256)S(1)} %dynamic-update-slice.11), channel_id=1, replica_groups=mesh['dom'=8,'col'=4] {'col'}, use_global_device_ids=true, to_apply=%add.1 | all-reduce | flops 256 | bytes 2048
  229.9 11.7 %cholesky.50 = f32[128,128]{1,0:T(8,128)S(1)} custom-call(f32[128,128]{1,0:T(8,128)S(1)} %cholesky.118), custom_call_target="Cholesky" | custom-call | tf_op jit(solution)/shard_map/jit(cholesky)/cholesky | solution.py:113
  241.7 9.8 %custom-call.16 = f32[1,128,128]{1,2,0:T(8,128)S(1)} custom-call(f32[1,128,128]{2,1,0:T(8,128)S(1)} %get-tuple-element.46), custom_call_target="InvertDiagBlocksLowerTriangular" | custom-call | tf_op jit(solution)/shard_map/jit(cholesky)/cholesky | solution.py:113
  252.0 11.7 %cholesky.105 = f32[128,128]{1,0:T(8,128)S(1)} custom-call(f32[128,128]{1,0:T(8,128)S(1)} %convolution_subtract_fusion), custom_call_target="Cholesky" | custom-call | tf_op jit(solution)/shard_map/jit(cholesky)/cholesky | solution.py:113
  266.5 4.1 %while.1 = (s32[]{:T(128)}, f32[256,256]{1,0:T(8,128)S(1)}, s32[2,2]{1,0:T(2,128)S(1)}, f32[2,128,128]{2,1,0:T(8,128)S(1)}, s32[]{:T(128)}) while((s32[]{:T(128)}, f32[256,256]{1,0:T(8,128)S(1)}, s32[2,2]{1,0:T(2,128)S(1)}, f32[2,128,128]{2,1,0:T(8,128)S(1)}, s32[]{:T(128)}) %tuple.40), condition=%wide.while_cond, body=%wide.while_body.sunk | while | flops 2 | bytes 131189 | solution.py:115
  270.5 19.9 %custom-call.17 = f32[2,128,128]{1,2,0:T(8,128)S(1)} custom-call(f32[2,128,128]{2,1,0:T(8,128)S(1)} %get-tuple-element.11), custom_call_target="InvertDiagBlocksLowerTriangular" | custom-call | tf_op jit(solution)/shard_map/triangular_solve | solution.py:115
  (80 shorter events, 31.4 us)
Async XLA Ops:
  20.1 39.8 %all-to-all-start = ((f32[1,8,256]{2,0,1:T(1,128)}), f32[1,8,256]{2,0,1:T(1,128)S(1)}, u32[]{:S(2)}, u32[]{:S(2)}) async-start(f32[1,8,256]{2,0,1:T(1,128)} %bitcast.11), calls=%async_computation | async-start | bytes 16384 | tf_op jit(solution)/shard_map/all_to_all | solution.py:91
  36.1 3.8 %copy-start.4 = (s32[64,2]{0,1:T(2,128)S(1)}, s32[64,2]{0,1:T(2,128)}, u32[]{:S(2)}) copy-start(s32[64,2]{0,1:T(2,128)} %param.9) | copy-start | bytes 1540
  47.8 3.8 %copy-start.1 = (bf16[64,64,320]{2,1,0:T(8,128)(2,1)S(1)}, bf16[64,64,320]{2,1,0:T(8,128)(2,1)}, u32[]{:S(2)}) copy-start(bf16[64,64,320]{2,1,0:T(8,128)(2,1)} %gather_fusion.1) | copy-start | bytes 7864324
  47.8 3.8 %copy-start.2 = (bf16[1,320,2048]{1,2,0:T(8,128)(2,1)S(1)}, bf16[1,320,2048]{1,2,0:T(8,128)(2,1)}, u32[]{:S(2)}) copy-start(bf16[1,320,2048]{1,2,0:T(8,128)(2,1)} %copy.32) | copy-start | bytes 3932164
  59.9 16.1 %all-to-all-start.1 = ((f32[64,8,256]{2,0,1:T(8,128)}), f32[64,8,256]{2,0,1:T(8,128)S(1)}, u32[]{:S(2)}, u32[]{:S(2)}) async-start(f32[64,8,256]{2,0,1:T(8,128)} %copy.35), calls=%async_computation.1 | async-start | bytes 1048576 | tf_op jit(solution)/shard_map/all_to_all | solution.py:89
  64.1 54.5 %all-gather.2.cloned.1.call-start = ((), (), s32[]{:S(2)}) async-start(), calls=%async_computation.3 | async-start | bytes 1310720 | tf_op jit(solution)/shard_map/all_gather | solution.py:101
  76.4 111.1 %copy-start.5 = (u32[32]{0:T(128)S(1)}, u32[32]{0:T(128)}, u32[]{:S(2)}) copy-start(u32[32]{0:T(128)} %constant.190) | copy-start | bytes 388
  97.8 90.9 %all-to-all-start.2 = ((f32[1,8,256]{2,0,1:T(1,128)}), f32[1,8,256]{2,0,1:T(1,128)S(1)}, u32[]{:S(2)}, u32[]{:S(2)}) async-start(f32[1,8,256]{2,0,1:T(1,128)} %bitcast.18), calls=%async_computation.2 | async-start | bytes 16384 | tf_op jit(solution)/shard_map/all_to_all | solution.py:90
  101.7 72.5 %all-reduce.4.cloned.1.call-start = ((), (), s32[]{:S(2)}) async-start(), calls=%async_computation.4 | async-start | bytes 131072 | tf_op jit(solution)/shard_map/psum | solution.py:108
  174.3 30.1 %collective-permute-start = (f32[64,256]{1,0:T(8,128)}, f32[64,256]{1,0:T(8,128)S(1)}, u32[]{:S(2)}, u32[]{:S(2)}) collective-permute-start(f32[64,256]{1,0:T(8,128)} %all-reduce.4.cloned.1.call-done), channel_id=1, source_target_pairs={{0,1},{1,2},{2,3},{3,0},{4,5},{5,6},{6,7},{7,4},{8,9},{9,10},{10,1... | collective-permute-start | bytes 196616 | tf_op jit(solution)/shard_map/ppermute | solution.py:26
  188.7 13.2 %copy-start.3 = (f32[64,256]{1,0:T(8,128)S(1)}, f32[64,256]{1,0:T(8,128)}, u32[]{:S(2)}) copy-start(f32[64,256]{1,0:T(8,128)} %all-reduce.4.cloned.1.call-done) | copy-start | bytes 196612
  201.9 90.3 %copy-start = (f32[1024]{0:T(1024)}, f32[1024]{0:T(1024)S(1)}, u32[]{:S(2)}) copy-start(f32[1024]{0:T(1024)S(1)} %scatter_fusion.1) | copy-start | bytes 12292
  202.0 27.2 %collective-permute-start.2 = (f32[64,256]{1,0:T(8,128)S(1)}, f32[64,256]{1,0:T(8,128)S(1)}, u32[]{:S(2)}, u32[]{:S(2)}) collective-permute-start(f32[64,256]{1,0:T(8,128)S(1)} %copy-done.3), channel_id=1, source_target_pairs={{1,0},{2,1},{3,2},{0,3},{5,4},{6,5},{7,6},{4,7},{9,8},{10,9},{11,1... | collective-permute-start | bytes 196616 | tf_op jit(solution)/shard_map/ppermute | solution.py:28
  204.4 24.8 %collective-permute-start.1 = (f32[64,256]{1,0:T(8,128)S(1)}, f32[64,256]{1,0:T(8,128)S(1)}, u32[]{:S(2)}, u32[]{:S(2)}) collective-permute-start(f32[64,256]{1,0:T(8,128)S(1)} %collective-permute-done), channel_id=1, source_target_pairs={{0,1},{1,2},{2,3},{3,0},{4,5},{5,6},{6,7},{7,4},{8,9},{9,10},{10,1... | collective-permute-start | bytes 196616 | tf_op jit(solution)/shard_map/ppermute | solution.py:26
Sparse Core Ops, SparseCore 0:
  89.1 29.4 all-gather.1
  121.7 52.5 all-reduce.3
